TPU v7x, 32 devices: a whole 2x2x4 slice. The times are simulated.
32 devices in a mesh: row: 8 (over z, y), col: 4 (over x, core).
Axes of the slice: x: 2, y: 2, z: 4, core: 2. Of those that a mesh axis runs over, the one named last changes fastest.
Arguments:
- weights: float32 [192, 16, 64, 64], P('row', 'col'), may hold values from 9.765625e-05 to 0.0029296875
- block_cols: int32 [192, 16], P('row'), may hold values from 0 to 191, as said below
- counts: int32 [192], P('row'), may hold values from 1 to 16, as said below
- near_null: float32 [192, 64], P('row'), may hold values from 0.5 to 2
- prior_ridge: float32 [192, 64], P('row'), may hold values from 0.1 to 1
Outputs:
- coarse_band: float32 [192, 128], P(('row', 'col'))
Inputs may be any that keep to these rules, and one draw needn't show every extreme that they name: `block_cols`: row i holds i in slot 0; its other slots hold distinct aggregates j with (j - i) modulo 192 between -21 and 21 and not 0; some row holds a neighbour at +21 and some at -21. Slots at or beyond a row's count are unused. `counts`: both ends are reached in every draw; the mean over the 24 rows of one index of row differs from index to index.
All inputs are finite; a program needn't handle non-finite values.
Results may differ from a plain program's by a relative error of at most 0.0003.
Values sent between devices are 32-bit elements; how exact they have to be, the bound alone decides.
No kernel may reach another device: no remote copies, remote signals or barrier semaphores. Data moves between devices by JAX's collectives and lax.ppermute only.
A program may use at most 64 MiB of HBM per device.

v0:
```python
import jax
import jax.numpy as jnp
from jax import lax
from jax.sharding import PartitionSpec as P

H = 21
BAND = 128
epsilon = 1e-06
relax_weight = 2.0 / 3.0


def with_halo(block, sides, width):
    for axis, dim in sides:
        count = lax.axis_size(axis)
        forward = [(i, i + 1) for i in range(count - 1)]
        forward.append((count - 1, 0))
        backward = [(target, source) for source, target in forward]
        low = lax.ppermute(
            lax.slice_in_dim(block, block.shape[dim] - width, None, axis=dim), axis, forward
        )
        high = lax.ppermute(lax.slice_in_dim(block, 0, width, axis=dim), axis, backward)
        block = jnp.concatenate([low, block, high], axis=dim)
    return block


def shifted_2(array, axis, by):
    devices = lax.axis_size(axis)
    return lax.ppermute(array, axis, [(i, (i + by) % devices) for i in range(devices)])


def band_form(tiles, tile_offsets):
    one_hot = (
        tile_offsets[..., None] + BAND // 2 == jnp.arange(BAND, dtype=jnp.int32)[None, None, :]
    ).astype(jnp.float32)
    return jnp.einsum("nkx,nkq->nxq", tiles, one_hot, precision=lax.Precision.HIGHEST)


def shift_table(amounts):
    band_pos = jnp.arange(BAND, dtype=jnp.int32)
    source = (band_pos[None, None, :] - amounts[:, None, None]) % BAND
    return (band_pos[None, :, None] == source).astype(jnp.float32)


def on_device(weights, block_cols, counts, near_null, prior_ridge):
    highest = lax.Precision.HIGHEST
    block_rows = weights.shape[0]
    slot_count = weights.shape[1]
    all_slots = block_cols.shape[1]
    total_blocks = block_rows * lax.axis_size("row")
    first_block = lax.axis_index("row") * block_rows
    column = lax.axis_index("col")
    local_rows = jnp.arange(block_rows, dtype=jnp.int32)
    offsets = (block_cols - (first_block + local_rows)[:, None] + H) % total_blocks - H
    mask_all = (jnp.arange(all_slots, dtype=jnp.int32)[None, :] < counts[:, None]).astype(
        jnp.float32
    )
    slot_start = column * slot_count
    mask_own = lax.dynamic_slice_in_dim(mask_all, slot_start, slot_count, 1)
    own_offsets = lax.dynamic_slice_in_dim(offsets, slot_start, slot_count, 1)
    slot_ids = slot_start + jnp.arange(slot_count, dtype=jnp.int32)
    degree_part = jnp.einsum("ikxy,ik->ix", weights, mask_own, precision=highest)
    degree = lax.psum(degree_part, "col") + prior_ridge
    unit_null = near_null / jnp.sqrt(
        jnp.sum(near_null * near_null, axis=1, keepdims=True) + epsilon
    )
    null_ext = with_halo(unit_null, (("row", 0),), H)
    targets = local_rows[:, None] + H + own_offsets
    near_rows = null_ext[targets]
    applied = jnp.einsum("ikxy,iky->ikx", weights, near_rows, precision=highest)
    own_term = (
        jnp.where(slot_ids == 0, 1.0 - relax_weight, 0.0).astype(jnp.float32)[None, :, None]
        * unit_null[:, None, :]
    )
    prolong = mask_own[:, :, None] * (own_term + relax_weight * applied / degree[:, None, :])
    part_band = band_form(prolong, own_offsets)
    whole_band = lax.psum(part_band, "col")
    ext_band = with_halo(whole_band, (("row", 0),), H)
    pick_hot = (
        offsets[..., None] + BAND // 2 == jnp.arange(BAND, dtype=jnp.int32)[None, None, :]
    ).astype(jnp.float32)
    full_slots = jnp.einsum("ixq,ikq->ikx", whole_band, pick_hot, precision=highest)
    own_band = ext_band[H : H + block_rows]
    summed = jnp.zeros(own_band.shape, jnp.float32)
    for slot_index in range(slot_count):
        picked = ext_band[targets[:, slot_index]]
        mover = shift_table(own_offsets[:, slot_index])
        rolled = jnp.einsum("iyp,ipq->iyq", picked, mover, precision=highest)
        step_term = jnp.einsum("ixy,iyq->ixq", weights[:, slot_index], rolled, precision=highest)
        summed = summed + mask_own[:, slot_index][:, None, None] * step_term
    applied_p = jnp.where(column == 0, degree[:, :, None] * own_band, 0.0) - summed
    contrib = jnp.einsum("ikx,ixq->ikq", full_slots, applied_p, precision=highest)
    pieces = []
    for slot_index in range(all_slots):
        mover = shift_table(-offsets[:, slot_index])
        pieces.append(jnp.einsum("ip,ipq->iq", contrib[:, slot_index], mover, precision=highest))
    shifted = jnp.stack(pieces, axis=1)
    destination = (local_rows[:, None] + H + offsets).reshape(-1)
    one_hot = (
        destination[:, None] == jnp.arange(block_rows + 2 * H, dtype=jnp.int32)[None, :]
    ).astype(jnp.float32)
    collected = jnp.einsum("nt,nq->tq", one_hot, shifted.reshape(-1, BAND), precision=highest)
    from_prev = shifted_2(collected[block_rows + H :], "row", 1)
    from_next = shifted_2(collected[:H], "row", -1)
    own_coarse = collected[H : block_rows + H]
    own_coarse = own_coarse.at[:H].add(from_prev)
    own_coarse = own_coarse.at[block_rows - H :].add(from_next)
    return lax.psum_scatter(own_coarse, "col", scatter_dimension=0, tiled=True)


def solution(mesh):
    placed = (P("row", "col", None, None), P("row", None), P("row"), P("row", None), P("row", None))
    return jax.shard_map(
        on_device, mesh=mesh, in_specs=placed, out_specs=P(("row", "col"), None), check_vma=False
    )
```

profile of v0, /device:TPU:0, one launch (start us, length us, event | category | flops | bytes accessed | tf_op | source)
XLA Modules:
  0.0 173.7 jit_solution(2995312101073054942)
XLA Ops:
  6.5 0.8 multiply_reduce_fusion
  8.2 3.0 %collective-permute-start = (f32[21,64]{1,0:T(8,128)S(1)}, f32[21,64]{1,0:T(8,128)S(1)}, u32[]{:S(2)}, u32[]{:S(2)}) collective-permute-start(f32[21,64]{1,0:T(8,128)S(1)} %get-tuple-element.39), channel_id=1, source_target_pairs={{0,4},{4,8},{8,12},{12,16},{16,20},{20,24},{24,28},{28,0},{1,5},{5... | collective-permute-start | bytes 16136 | tf_op jit(solution)/shard_map/ppermute | solution.py:18
  11.2 3.1 %collective-permute-start.1 = (f32[21,64]{1,0:T(8,128)S(1)}, f32[21,64]{1,0:T(8,128)S(1)}, u32[]{:S(2)}, u32[]{:S(2)}) collective-permute-start(f32[21,64]{1,0:T(8,128)S(1)} %get-tuple-element.40), channel_id=1, source_target_pairs={{4,0},{8,4},{12,8},{16,12},{20,16},{24,20},{28,24},{0,28},{5,1},{9... | collective-permute-start | bytes 16136 | tf_op jit(solution)/shard_map/ppermute | solution.py:21
  21.9 2.9 %reduce_sum.19 = f32[24,4,64]{2,1,0:T(4,128)S(1)} reduce(f32[24,4,64,64]{3,2,1,0:T(8,128)} %param.9, f32[]{:T(128)} %constant.208.clone.1), dimensions={3}, to_apply=%region_1.2 | reduce | flops 387072 | bytes 1597444 | tf_op jit(solution)/shard_map/ikxy,ik->ix/reduce_sum | solution.py:61
  25.1 10.6 %psum.14 = f32[24,64]{1,0:T(8,128)S(1)} all-reduce(f32[24,64]{1,0:T(8,128)S(1)} %bitcast.240), channel_id=1, replica_groups=mesh['row'=8,'col'=4] {'col'}, use_global_device_ids=true, to_apply=%region_2.3 | all-reduce | flops 1536 | bytes 12288 | tf_op jit(solution)/shard_map/psum | solution.py:62
  36.4 5.0 %fusion.175 = f32[24,4,1,64]{3,2,1,0:T(1,128)S(1)} fusion(f32[24,4,64,1]{2,3,1,0:T(1,128)S(1)} %bitcast.239, f32[24,4,64,64]{3,2,1,0:T(8,128)S(1)} %copy-done), kind=kOutput, calls=%fused_computation.338 | convolution fusion | flops 4718592 | bytes 1622016 | tf_op jit(solution)/shard_map/ikxy,iky->ikx/dot_general | solution.py:69
  41.4 1.8 %fusion.57 = f32[24,64,128]{2,1,0:T(8,128)} fusion(f32[24,4,64]{2,1,0:T(4,128)S(1)} %bitcast.238, s32[24,4]{1,0:T(8,128)S(1)} %copy.19, f32[24,64]{1,0:T(8,128)S(1)} %add.346, f32[24,64]{1,0:T(8,128)S(1)} %broadcast_divide_fusion, f32[4]{0:T(128)S(1)} %copy-done.16, f32[24,4]{1,0:T(8,128)S(1)} %copy.17), kind=kOutput, calls=%fused_computation.90 | convolution fusion | flops 9480192 | bytes 824080 | tf_op jit(solution)/shard_map/nkx,nkq->nxq/dot_general | solution.py:35
  44.5 32.1 %all-reduce.3.cloned.1.call-done = f32[24,64,128]{2,1,0:T(8,128)} async-done(((f32[24,64,128]{2,1,0:T(8,128)}), f32[24,64,128]{2,1,0:T(8,128)}) %all-reduce.3.cloned.1.call-update) | async-done | bytes 786448 | tf_op jit(solution)/shard_map/psum | solution.py:76
  76.6 1.5 fusion.172
  78.0 1.5 collective-permute-start.2
  80.2 3.2 %collective-permute-start.3 = (f32[21,64,128]{2,1,0:T(8,128)S(1)}, f32[21,64,128]{2,1,0:T(8,128)S(1)}, u32[]{:S(2)}, u32[]{:S(2)}) collective-permute-start(f32[21,64,128]{2,1,0:T(8,128)S(1)} %get-tuple-element.35), channel_id=1, source_target_pairs={{4,0},{8,4},{12,8},{16,12},{20,16},{24,20},{28,24},{0,28},{5,1},{9... | collective-permute-start | bytes 2064392 | tf_op jit(solution)/shard_map/ppermute | solution.py:21
  84.8 23.1 %collective-permute-done.2 = f32[21,64,128]{2,1,0:T(8,128)S(1)} collective-permute-done((f32[21,64,128]{2,1,0:T(8,128)S(1)}, f32[21,64,128]{2,1,0:T(8,128)S(1)}, u32[]{:S(2)}, u32[]{:S(2)}) %collective-permute-start.2) | collective-permute-done | bytes 688160 | tf_op jit(solution)/shard_map/ppermute | solution.py:18
  107.9 0.9 constant_dynamic-update-slice_fusion.2
  108.8 1.0 constant_dynamic-update-slice_fusion.1
  109.8 1.0 collective-permute-done.3
  110.8 0.9 constant_dynamic-update-slice_fusion
  111.7 3.2 %gather_fusion.1 = f32[24,64,128]{2,1,0:T(8,128)} fusion(f32[66,64,128]{2,1,0:T(8,128)} %constant_dynamic-update-slice_fusion, s32[1024]{0:T(1024)} %pad_clamp_fusion.3), kind=kCustom, calls=%fused_computation.1 | custom fusion | bytes 1572960 | tf_op jit(solution)/shard_map/gather | solution.py:85
  114.9 3.2 %gather_fusion.2 = f32[24,64,128]{2,1,0:T(8,128)} fusion(f32[66,64,128]{2,1,0:T(8,128)} %constant_dynamic-update-slice_fusion, s32[1024]{0:T(1024)} %pad_clamp_fusion.2), kind=kCustom, calls=%fused_computation.2 | custom fusion | bytes 1572960 | tf_op jit(solution)/shard_map/gather | solution.py:85
  118.1 3.2 %gather_fusion.3 = f32[24,64,128]{2,1,0:T(8,128)} fusion(f32[66,64,128]{2,1,0:T(8,128)} %constant_dynamic-update-slice_fusion, s32[1024]{0:T(1024)} %pad_clamp_fusion.1), kind=kCustom, calls=%fused_computation.3 | custom fusion | bytes 1572960 | tf_op jit(solution)/shard_map/gather | solution.py:85
  121.4 3.2 %gather_fusion.4 = f32[24,64,128]{2,1,0:T(8,128)} fusion(f32[66,64,128]{2,1,0:T(8,128)} %constant_dynamic-update-slice_fusion, s32[1024]{0:T(1024)} %pad_clamp_fusion), kind=kCustom, calls=%fused_computation.4 | custom fusion | bytes 1572960 | tf_op jit(solution)/shard_map/gather | solution.py:85
  124.6 2.1 %fusion = f32[24,64,128]{2,1,0:T(8,128)S(1)} fusion(f32[24,64,128]{2,1,0:T(8,128)} %gather_fusion.1, s32[24,128]{1,0:T(8,128)S(1)} %add_select_fusion.19), kind=kOutput, calls=%fused_computation.25 | convolution fusion | flops 302383104 | bytes 1585152 | tf_op jit(solution)/shard_map/iyp,ipq->iyq/dot_general | solution.py:87
  126.7 0.9 convolution_multiply_fusion.3
  127.8 0.9 fusion.1
  128.7 0.9 fusion.2
  129.7 0.9 fusion.3
  130.6 0.9 fusion.24
  131.5 0.9 fusion.23
  132.7 1.0 fusion.22
  134.5 0.8 fusion.10
  135.3 0.8 fusion.11
  136.1 0.8 fusion.12
  136.9 1.0 fusion.13
  138.0 0.8 fusion.14
  138.8 0.8 fusion.15
  139.6 0.8 fusion.16
  140.4 0.8 fusion.17
  141.2 0.8 fusion.18
  142.0 0.8 fusion.19
  142.9 0.8 fusion.6
  143.7 0.8 fusion.7
  144.5 0.8 fusion.8
  145.3 0.8 fusion.9
  146.1 0.8 fusion.5
  146.9 0.8 fusion.4
  148.5 1.5 collective-permute-start.4
  151.3 3.3 %collective-permute-start.5 = (f32[21,128]{1,0:T(8,128)S(1)}, f32[21,128]{1,0:T(8,128)S(1)}, u32[]{:S(2)}, u32[]{:S(2)}) collective-permute-start(f32[21,128]{1,0:T(8,128)S(1)} %get-tuple-element.37), channel_id=1, source_target_pairs={{0,28},{4,0},{8,4},{12,8},{16,12},{20,16},{24,20},{28,24},{1,29},{... | collective-permute-start | bytes 32264 | tf_op jit(solution)/shard_map/ppermute | solution.py:28
  155.1 0.8 collective-permute-done.5
  156.2 10.1 %all-reduce = f32[24,128]{1,0:T(8,128)S(1)} all-reduce(f32[24,128]{1,0:T(8,128)S(1)} %scatter-add.9), channel_id=2, replica_groups=mesh['row'=8,'col'=4] {'col'}, use_global_device_ids=true, to_apply=%region_4.5.clone | all-reduce | flops 3072 | bytes 24576
  (104 shorter events, 16.6 us)
Async XLA Ops:
  6.5 70.0 %all-reduce.3.cloned.1.call-start = ((), (), s32[]{:S(2)}) async-start(), calls=%async_computation | async-start | bytes 1572864 | tf_op jit(solution)/shard_map/psum | solution.py:76
  8.2 27.5 %collective-permute-start = (f32[21,64]{1,0:T(8,128)S(1)}, f32[21,64]{1,0:T(8,128)S(1)}, u32[]{:S(2)}, u32[]{:S(2)}) collective-permute-start(f32[21,64]{1,0:T(8,128)S(1)} %get-tuple-element.39), channel_id=1, source_target_pairs={{0,4},{4,8},{8,12},{12,16},{16,20},{20,24},{24,28},{28,0},{1,5},{5... | collective-permute-start | bytes 16136 | tf_op jit(solution)/shard_map/ppermute | solution.py:18
  11.2 24.5 %collective-permute-start.1 = (f32[21,64]{1,0:T(8,128)S(1)}, f32[21,64]{1,0:T(8,128)S(1)}, u32[]{:S(2)}, u32[]{:S(2)}) collective-permute-start(f32[21,64]{1,0:T(8,128)S(1)} %get-tuple-element.40), channel_id=1, source_target_pairs={{4,0},{8,4},{12,8},{16,12},{20,16},{24,20},{28,24},{0,28},{5,1},{9... | collective-permute-start | bytes 16136 | tf_op jit(solution)/shard_map/ppermute | solution.py:21
  21.9 13.8 %copy-start.11 = (f32[24,64]{1,0:T(8,128)S(1)}, f32[24,64]{1,0:T(8,128)}, u32[]{:S(2)}) copy-start(f32[24,64]{1,0:T(8,128)} %param.13) | copy-start | bytes 18436
  21.9 14.4 %copy-start = (f32[24,4,64,64]{3,2,1,0:T(8,128)S(1)}, f32[24,4,64,64]{3,2,1,0:T(8,128)}, u32[]{:S(2)}) copy-start(f32[24,4,64,64]{3,2,1,0:T(8,128)} %param.9) | copy-start | bytes 4718596
  36.4 5.0 %copy-start.16 = (f32[4]{0:T(128)S(1)}, f32[4]{0:T(128)}, u32[]{:S(2)}) copy-start(f32[4]{0:T(128)} %compare_select_fusion.5) | copy-start | bytes 52
  76.6 7.5 %copy-start.1 = (f32[24,64,128]{2,1,0:T(8,128)S(1)}, f32[24,64,128]{2,1,0:T(8,128)}, u32[]{:S(2)}) copy-start(f32[24,64,128]{2,1,0:T(8,128)} %all-reduce.3.cloned.1.call-done) | copy-start | bytes 2359300
  78.0 29.9 %collective-permute-start.2 = (f32[21,64,128]{2,1,0:T(8,128)S(1)}, f32[21,64,128]{2,1,0:T(8,128)S(1)}, u32[]{:S(2)}, u32[]{:S(2)}) collective-permute-start(f32[21,64,128]{2,1,0:T(8,128)S(1)} %get-tuple-element.36), channel_id=1, source_target_pairs={{0,4},{4,8},{8,12},{12,16},{16,20},{20,24},{24,28},{28,0},{1,5},{5... | collective-permute-start | bytes 2064392 | tf_op jit(solution)/shard_map/ppermute | solution.py:18
  80.2 30.5 %collective-permute-start.3 = (f32[21,64,128]{2,1,0:T(8,128)S(1)}, f32[21,64,128]{2,1,0:T(8,128)S(1)}, u32[]{:S(2)}, u32[]{:S(2)}) collective-permute-start(f32[21,64,128]{2,1,0:T(8,128)S(1)} %get-tuple-element.35), channel_id=1, source_target_pairs={{4,0},{8,4},{12,8},{16,12},{20,16},{24,20},{28,24},{0,28},{5,1},{9... | collective-permute-start | bytes 2064392 | tf_op jit(solution)/shard_map/ppermute | solution.py:21
  121.4 5.3 %copy-start.13 = (f32[24]{0:T(128)S(1)}, f32[24]{0:T(128)}, u32[]{:S(2)}) copy-start(f32[24]{0:T(128)} %get-tuple-element.61) | copy-start | bytes 292
  126.6 1.1 copy-start.5
  126.6 2.1 %copy-start.4 = (f32[24,64,128]{2,1,0:T(8,128)S(1)}, f32[24,64,128]{2,1,0:T(8,128)}, u32[]{:S(2)}) copy-start(f32[24,64,128]{2,1,0:T(8,128)} %gather_fusion.3) | copy-start | bytes 2359300
  127.8 1.9 %copy-start.3 = (f32[24,64,128]{2,1,0:T(8,128)S(1)}, f32[24,64,128]{2,1,0:T(8,128)}, u32[]{:S(2)}) copy-start(f32[24,64,128]{2,1,0:T(8,128)} %gather_fusion.4) | copy-start | bytes 2359300
  128.7 1.9 %copy-start.15 = (f32[24]{0:T(128)S(1)}, f32[24]{0:T(128)}, u32[]{:S(2)}) copy-start(f32[24]{0:T(128)} %get-tuple-element.60) | copy-start | bytes 292
  130.6 0.9 copy-start.14
  131.5 1.1 copy-start.2
  131.5 1.1 copy-start.12
  138.8 4.9 %copy-start.6 = (s32[24,128]{1,0:T(8,128)S(1)}, s32[24,128]{1,0:T(8,128)}, u32[]{:S(2)}) copy-start(s32[24,128]{1,0:T(8,128)} %add_select_fusion.12) | copy-start | bytes 36868
  139.6 4.9 %copy-start.7 = (s32[24,128]{1,0:T(8,128)S(1)}, s32[24,128]{1,0:T(8,128)}, u32[]{:S(2)}) copy-start(s32[24,128]{1,0:T(8,128)} %add_select_fusion.11) | copy-start | bytes 36868
  140.4 4.9 %copy-start.8 = (s32[24,128]{1,0:T(8,128)S(1)}, s32[24,128]{1,0:T(8,128)}, u32[]{:S(2)}) copy-start(s32[24,128]{1,0:T(8,128)} %add_select_fusion.10) | copy-start | bytes 36868
  141.2 4.9 %copy-start.9 = (s32[24,128]{1,0:T(8,128)S(1)}, s32[24,128]{1,0:T(8,128)}, u32[]{:S(2)}) copy-start(s32[24,128]{1,0:T(8,128)} %add_select_fusion.14) | copy-start | bytes 36868
  142.0 4.9 %copy-start.10 = (s32[24,128]{1,0:T(8,128)S(1)}, s32[24,128]{1,0:T(8,128)}, u32[]{:S(2)}) copy-start(s32[24,128]{1,0:T(8,128)} %add_select_fusion.15) | copy-start | bytes 36868
  143.7 6.4 %copy-start.17 = (u32[32]{0:T(128)S(1)}, u32[32]{0:T(128)}, u32[]{:S(2)}) copy-start(u32[32]{0:T(128)} %constant.218) | copy-start | bytes 388
  148.5 6.4 %collective-permute-start.4 = (f32[21,128]{1,0:T(8,128)S(1)}, f32[21,128]{1,0:T(8,128)S(1)}, u32[]{:S(2)}, u32[]{:S(2)}) collective-permute-start(f32[21,128]{1,0:T(8,128)S(1)} %get-tuple-element.38), channel_id=1, source_target_pairs={{0,4},{4,8},{8,12},{12,16},{16,20},{20,24},{24,28},{28,0},{1,5},{5... | collective-permute-start | bytes 32264 | tf_op jit(solution)/shard_map/ppermute | solution.py:28
  151.3 4.7 %collective-permute-start.5 = (f32[21,128]{1,0:T(8,128)S(1)}, f32[21,128]{1,0:T(8,128)S(1)}, u32[]{:S(2)}, u32[]{:S(2)}) collective-permute-start(f32[21,128]{1,0:T(8,128)S(1)} %get-tuple-element.37), channel_id=1, source_target_pairs={{0,28},{4,0},{8,4},{12,8},{16,12},{20,16},{24,20},{28,24},{1,29},{... | collective-permute-start | bytes 32264 | tf_op jit(solution)/shard_map/ppermute | solution.py:28
Sparse Core Ops, SparseCore 0:
  43.3 33.2 all-reduce.2
where the time goes:
time: 174 us
  waiting for transfers between devices  57.4 us (33%)
  matrix products  30.7 us (18%)
  local copies, waits for them, and re-layouts  21.4 us (12%)
  blocking collectives  20.7 us (12%)
  starting transfers between devices  15.8 us (9%)
  between operations  14.4 us (8%)
  other arithmetic  13.5 us (8%)
    psum x1, waiting for transfers between devices, on_device(): whole_band = lax.psum(part_band, 'col')  32.1 us
    ppermute x2, waiting for transfers between devices, with_halo(): lax.ppermute(lax.slice_in_dim(block, block.shape[dim] - width, None, axis...  23.1 us
    dot_general x16, matrix products, on_device(): jnp.einsum('ip,ipq->iq', contrib[:, slot_index], mover, precision=highest)  13.2 us
    gather x4, local copies, waits for them, and re-layouts, on_device(): picked = ext_band[targets[:, slot_index]]  12.9 us
    psum x1, blocking collectives, on_device(): degree = lax.psum(degree_part, 'col') + prior_ridge  10.6 us
    unnamed x1, blocking collectives  10.1 us
    ppermute x2, starting transfers between devices, with_halo(): lax.ppermute(lax.slice_in_dim(block, 0, width, axis=dim), axis, backward)  6.35 us
    dot_general x1, matrix products, on_device(): applied = jnp.einsum('ikxy,iky->ikx', weights, near_rows, precision=highest)  4.97 us
  transfers between devices with their start and end apart: 7, of which 5 were waited for; matrix products, arithmetic and copies ran while one was open for 10% of the time, Pallas kernels for 0%

commit v1 on v0

--- a/solution.py
+++ b/solution.py
@@ -73,7 +73,8 @@
     )
     prolong = mask_own[:, :, None] * (own_term + relax_weight * applied / degree[:, None, :])
     part_band = band_form(prolong, own_offsets)
-    whole_band = lax.psum(part_band, "col")
+    shards = lax.all_gather(part_band, "col")
+    whole_band = jnp.sum(shards, axis=0)
     ext_band = with_halo(whole_band, (("row", 0),), H)
     pick_hot = (
         offsets[..., None] + BAND // 2 == jnp.arange(BAND, dtype=jnp.int32)[None, None, :]

time: 174 us -> 169 us (0.971)
  waiting for transfers between devices: 57.4 us -> 50.1 us
  other arithmetic: 13.5 us -> 17.6 us
  local copies, waits for them, and re-layouts: 21.4 us -> 18.7 us
    psum x1 -> x0, waiting for transfers between devices: 32.1 us -> none  [on_device(): whole_band = lax.psum(part_band, 'col')]
    all_gather x0 -> x1, waiting for transfers between devices: none -> 22.2 us  [on_device(): shards = lax.all_gather(part_band, 'col')]
    reduce_sum x0 -> x1, other arithmetic: none -> 3.13 us  [on_device(): whole_band = jnp.sum(shards, axis=0)]
    unnamed x40 -> x36, local copies, waits for them, and re-layouts: 3.59 us -> 1.72 us
  transfers between devices with their start and end apart: 7 -> 7, of which waited for: 5 -> 5; matrix products, arithmetic and copies ran while one was open for 10% -> 9% of each run, Pallas kernels for 0% -> 0%
where the time goes in v1:
time: 169 us; the launch traced here: 168 us
  waiting for transfers between devices  50.1 us (30%)
  matrix products  30.7 us (18%)
  blocking collectives  20.8 us (12%)
  local copies, waits for them, and re-layouts  18.7 us (11%)
  other arithmetic  17.6 us (10%)
  starting transfers between devices  15.8 us (9%)
  between operations  14.4 us (9%)
    ppermute x2, waiting for transfers between devices, with_halo(): lax.ppermute(lax.slice_in_dim(block, block.shape[dim] - width, None, axis...  24.5 us
    all_gather x1, waiting for transfers between devices, on_device(): shards = lax.all_gather(part_band, 'col')  22.2 us
    dot_general x16, matrix products, on_device(): jnp.einsum('ip,ipq->iq', contrib[:, slot_index], mover, precision=highest)  13.2 us
    gather x4, local copies, waits for them, and re-layouts, on_device(): picked = ext_band[targets[:, slot_index]]  12.9 us
    psum x1, blocking collectives, on_device(): degree = lax.psum(degree_part, 'col') + prior_ridge  10.6 us
    unnamed x1, blocking collectives  10.2 us
    ppermute x2, starting transfers between devices, with_halo(): lax.ppermute(lax.slice_in_dim(block, 0, width, axis=dim), axis, backward)  6.35 us
    dot_general x1, matrix products, on_device(): applied = jnp.einsum('ikxy,iky->ikx', weights, near_rows, precision=highest)  4.98 us
  transfers between devices with their start and end apart: 7, of which 5 were waited for; matrix products, arithmetic and copies ran while one was open for 9% of the time, Pallas kernels for 0%

profile of v1, /device:TPU:0, one launch (start us, length us, event | category | flops | bytes accessed | tf_op | source)
XLA Modules:
  0.0 167.9 jit_solution(6025646280545218956)
XLA Ops:
  6.5 0.8 multiply_reduce_fusion
  7.4 0.8 broadcast_divide_fusion
  8.2 3.0 %collective-permute-start = (f32[21,64]{1,0:T(8,128)S(1)}, f32[21,64]{1,0:T(8,128)S(1)}, u32[]{:S(2)}, u32[]{:S(2)}) collective-permute-start(f32[21,64]{1,0:T(8,128)S(1)} %get-tuple-element.39), channel_id=1, source_target_pairs={{0,4},{4,8},{8,12},{12,16},{16,20},{20,24},{24,28},{28,0},{1,5},{5... | collective-permute-start | bytes 16136 | tf_op jit(solution)/shard_map/ppermute | solution.py:18
  11.2 3.1 %collective-permute-start.1 = (f32[21,64]{1,0:T(8,128)S(1)}, f32[21,64]{1,0:T(8,128)S(1)}, u32[]{:S(2)}, u32[]{:S(2)}) collective-permute-start(f32[21,64]{1,0:T(8,128)S(1)} %get-tuple-element.40), channel_id=1, source_target_pairs={{4,0},{8,4},{12,8},{16,12},{20,16},{24,20},{28,24},{0,28},{5,1},{9... | collective-permute-start | bytes 16136 | tf_op jit(solution)/shard_map/ppermute | solution.py:21
  18.0 2.9 %reduce_sum.28 = f32[24,4,64]{2,1,0:T(4,128)S(1)} reduce(f32[24,4,64,64]{3,2,1,0:T(8,128)} %param.9, f32[]{:T(128)} %constant.208.clone.1), dimensions={3}, to_apply=%region_1.2 | reduce | flops 387072 | bytes 1597444 | tf_op jit(solution)/shard_map/ikxy,ik->ix/reduce_sum | solution.py:61
  21.2 10.6 %psum.7 = f32[24,64]{1,0:T(8,128)S(1)} all-reduce(f32[24,64]{1,0:T(8,128)S(1)} %bitcast.242), channel_id=1, replica_groups=mesh['row'=8,'col'=4] {'col'}, use_global_device_ids=true, to_apply=%region_2.3 | all-reduce | flops 1536 | bytes 12288 | tf_op jit(solution)/shard_map/psum | solution.py:62
  32.4 5.0 %fusion.175 = f32[24,4,1,64]{3,2,1,0:T(1,128)S(1)} fusion(f32[24,4,64,1]{2,3,1,0:T(1,128)S(1)} %bitcast.241, f32[24,4,64,64]{3,2,1,0:T(8,128)S(1)} %copy-done), kind=kOutput, calls=%fused_computation.336 | convolution fusion | flops 4718592 | bytes 1622016 | tf_op jit(solution)/shard_map/ikxy,iky->ikx/dot_general | solution.py:69
  37.4 1.8 %fusion.57 = f32[24,64,128]{2,1,0:T(8,128)} fusion(f32[24,4,64]{2,1,0:T(4,128)S(1)} %bitcast.240, s32[24,4]{1,0:T(8,128)S(1)} %copy.19, f32[24,64]{1,0:T(8,128)S(1)} %add.344, f32[24,64]{1,0:T(8,128)S(1)} %broadcast_divide_fusion, f32[4]{0:T(128)S(1)} %compare_select_fusion.5, f32[24,4]{1,0:T(8,128)S(1)} %copy.17), kind=kOutput, calls=%fused_computation.91 | convolution fusion | flops 9480192 | bytes 824080 | tf_op jit(solution)/shard_map/nkx,nkq->nxq/dot_general | solution.py:35
  44.0 22.2 %all-gather.3.cloned.1.call-done = f32[96,64,128]{2,1,0:T(8,128)} async-done(((f32[24,64,128]{2,1,0:T(8,128)}), f32[96,64,128]{2,1,0:T(8,128)}) %all-gather.3.cloned.1.call-update) | async-done | bytes 3145744 | tf_op jit(solution)/shard_map/all_gather | solution.py:76
  66.2 3.1 %reduce_sum.29 = f32[24,64,128]{2,1,0:T(8,128)} reduce(f32[4,24,64,128]{3,2,1,0:T(8,128)} %bitcast.238, f32[]{:T(128)} %constant.208.clone.1), dimensions={0}, to_apply=%region_3.4 | reduce | flops 589824 | bytes 3932164 | tf_op jit(solution)/shard_map/reduce_sum | solution.py:77
  69.3 1.5 fusion.172
  70.8 1.5 collective-permute-start.2
  72.3 3.2 %collective-permute-start.3 = (f32[21,64,128]{2,1,0:T(8,128)S(1)}, f32[21,64,128]{2,1,0:T(8,128)S(1)}, u32[]{:S(2)}, u32[]{:S(2)}) collective-permute-start(f32[21,64,128]{2,1,0:T(8,128)S(1)} %get-tuple-element.36), channel_id=1, source_target_pairs={{4,0},{8,4},{12,8},{16,12},{20,16},{24,20},{28,24},{0,28},{5,1},{9... | collective-permute-start | bytes 2064392 | tf_op jit(solution)/shard_map/ppermute | solution.py:21
  77.6 24.5 %collective-permute-done.2 = f32[21,64,128]{2,1,0:T(8,128)S(1)} collective-permute-done((f32[21,64,128]{2,1,0:T(8,128)S(1)}, f32[21,64,128]{2,1,0:T(8,128)S(1)}, u32[]{:S(2)}, u32[]{:S(2)}) %collective-permute-start.2) | collective-permute-done | bytes 688160 | tf_op jit(solution)/shard_map/ppermute | solution.py:18
  102.1 2.2 %collective-permute-done.3 = f32[21,64,128]{2,1,0:T(8,128)S(1)} collective-permute-done((f32[21,64,128]{2,1,0:T(8,128)S(1)}, f32[21,64,128]{2,1,0:T(8,128)S(1)}, u32[]{:S(2)}, u32[]{:S(2)}) %collective-permute-start.3) | collective-permute-done | bytes 688160 | tf_op jit(solution)/shard_map/ppermute | solution.py:21
  104.3 1.5 pad_maximum_fusion
  105.8 3.2 %gather_fusion.1 = f32[24,64,128]{2,1,0:T(8,128)} fusion(f32[66,64,128]{2,1,0:T(8,128)} %pad_maximum_fusion, s32[1024]{0:T(1024)} %pad_clamp_fusion.3), kind=kCustom, calls=%fused_computation.1 | custom fusion | bytes 1572960 | tf_op jit(solution)/shard_map/gather | solution.py:86
  109.0 3.2 %gather_fusion.2 = f32[24,64,128]{2,1,0:T(8,128)} fusion(f32[66,64,128]{2,1,0:T(8,128)} %pad_maximum_fusion, s32[1024]{0:T(1024)} %pad_clamp_fusion.2), kind=kCustom, calls=%fused_computation.2 | custom fusion | bytes 1572960 | tf_op jit(solution)/shard_map/gather | solution.py:86
  112.3 3.2 %gather_fusion.3 = f32[24,64,128]{2,1,0:T(8,128)} fusion(f32[66,64,128]{2,1,0:T(8,128)} %pad_maximum_fusion, s32[1024]{0:T(1024)} %pad_clamp_fusion.1), kind=kCustom, calls=%fused_computation.3 | custom fusion | bytes 1572960 | tf_op jit(solution)/shard_map/gather | solution.py:86
  115.5 3.2 %gather_fusion.4 = f32[24,64,128]{2,1,0:T(8,128)} fusion(f32[66,64,128]{2,1,0:T(8,128)} %pad_maximum_fusion, s32[1024]{0:T(1024)} %pad_clamp_fusion), kind=kCustom, calls=%fused_computation.4 | custom fusion | bytes 1572960 | tf_op jit(solution)/shard_map/gather | solution.py:86
  118.7 2.1 %fusion = f32[24,64,128]{2,1,0:T(8,128)S(1)} fusion(f32[24,64,128]{2,1,0:T(8,128)} %gather_fusion.1, s32[24,128]{1,0:T(8,128)S(1)} %add_select_fusion.19), kind=kOutput, calls=%fused_computation.26 | convolution fusion | flops 302383104 | bytes 1585152 | tf_op jit(solution)/shard_map/iyp,ipq->iyq/dot_general | solution.py:88
  120.8 0.9 convolution_multiply_fusion.3
  121.9 0.9 fusion.1
  122.9 0.9 fusion.2
  123.8 0.9 fusion.3
  124.7 0.9 fusion.24
  125.7 0.9 fusion.23
  126.8 1.0 fusion.22
  127.8 0.8 fusion.177
  128.6 0.8 fusion.10
  129.4 0.8 fusion.11
  130.2 0.8 fusion.12
  131.0 1.0 fusion.13
  132.1 0.8 fusion.14
  132.9 0.8 fusion.15
  133.7 0.8 fusion.16
  134.5 0.8 fusion.17
  135.3 0.8 fusion.18
  136.2 0.8 fusion.19
  137.0 0.8 fusion.6
  137.8 0.8 fusion.7
  138.6 0.8 fusion.8
  139.4 0.8 fusion.9
  140.3 0.8 fusion.5
  141.1 0.8 fusion.4
  144.2 4.5 %collective-permute-start.5 = (f32[21,128]{1,0:T(8,128)S(1)}, f32[21,128]{1,0:T(8,128)S(1)}, u32[]{:S(2)}, u32[]{:S(2)}) collective-permute-start(f32[21,128]{1,0:T(8,128)S(1)} %get-tuple-element.37), channel_id=1, source_target_pairs={{0,28},{4,0},{8,4},{12,8},{16,12},{20,16},{24,20},{28,24},{1,29},{... | collective-permute-start | bytes 32264 | tf_op jit(solution)/shard_map/ppermute | solution.py:28
  149.3 0.8 collective-permute-done.5
  150.3 10.2 %all-reduce = f32[24,128]{1,0:T(8,128)S(1)} all-reduce(f32[24,128]{1,0:T(8,128)S(1)} %scatter-add.9), channel_id=3, replica_groups=mesh['row'=8,'col'=4] {'col'}, use_global_device_ids=true, to_apply=%region_4.5.clone | all-reduce | flops 3072 | bytes 24576
  (101 shorter events, 14.8 us)
Async XLA Ops:
  6.5 59.6 %all-gather.3.cloned.1.call-start = ((), (), s32[]{:S(2)}) async-start(), calls=%async_computation | async-start | bytes 3932160 | tf_op jit(solution)/shard_map/all_gather | solution.py:76
  8.2 23.6 %collective-permute-start = (f32[21,64]{1,0:T(8,128)S(1)}, f32[21,64]{1,0:T(8,128)S(1)}, u32[]{:S(2)}, u32[]{:S(2)}) collective-permute-start(f32[21,64]{1,0:T(8,128)S(1)} %get-tuple-element.39), channel_id=1, source_target_pairs={{0,4},{4,8},{8,12},{12,16},{16,20},{20,24},{24,28},{28,0},{1,5},{5... | collective-permute-start | bytes 16136 | tf_op jit(solution)/shard_map/ppermute | solution.py:18
  11.2 20.6 %collective-permute-start.1 = (f32[21,64]{1,0:T(8,128)S(1)}, f32[21,64]{1,0:T(8,128)S(1)}, u32[]{:S(2)}, u32[]{:S(2)}) collective-permute-start(f32[21,64]{1,0:T(8,128)S(1)} %get-tuple-element.40), channel_id=1, source_target_pairs={{4,0},{8,4},{12,8},{16,12},{20,16},{24,20},{28,24},{0,28},{5,1},{9... | collective-permute-start | bytes 16136 | tf_op jit(solution)/shard_map/ppermute | solution.py:21
  18.0 13.8 %copy-start.11 = (f32[24,64]{1,0:T(8,128)S(1)}, f32[24,64]{1,0:T(8,128)}, u32[]{:S(2)}) copy-start(f32[24,64]{1,0:T(8,128)} %param.13) | copy-start | bytes 18436
  18.0 14.4 %copy-start = (f32[24,4,64,64]{3,2,1,0:T(8,128)S(1)}, f32[24,4,64,64]{3,2,1,0:T(8,128)}, u32[]{:S(2)}) copy-start(f32[24,4,64,64]{3,2,1,0:T(8,128)} %param.9) | copy-start | bytes 4718596
  69.3 7.5 %copy-start.1 = (f32[24,64,128]{2,1,0:T(8,128)S(1)}, f32[24,64,128]{2,1,0:T(8,128)}, u32[]{:S(2)}) copy-start(f32[24,64,128]{2,1,0:T(8,128)} %reduce_sum.29) | copy-start | bytes 2359300
  70.8 31.4 %collective-permute-start.2 = (f32[21,64,128]{2,1,0:T(8,128)S(1)}, f32[21,64,128]{2,1,0:T(8,128)S(1)}, u32[]{:S(2)}, u32[]{:S(2)}) collective-permute-start(f32[21,64,128]{2,1,0:T(8,128)S(1)} %get-tuple-element.35), channel_id=1, source_target_pairs={{0,4},{4,8},{8,12},{12,16},{16,20},{20,24},{24,28},{28,0},{1,5},{5... | collective-permute-start | bytes 2064392 | tf_op jit(solution)/shard_map/ppermute | solution.py:18
  72.3 32.0 %collective-permute-start.3 = (f32[21,64,128]{2,1,0:T(8,128)S(1)}, f32[21,64,128]{2,1,0:T(8,128)S(1)}, u32[]{:S(2)}, u32[]{:S(2)}) collective-permute-start(f32[21,64,128]{2,1,0:T(8,128)S(1)} %get-tuple-element.36), channel_id=1, source_target_pairs={{4,0},{8,4},{12,8},{16,12},{20,16},{24,20},{28,24},{0,28},{5,1},{9... | collective-permute-start | bytes 2064392 | tf_op jit(solution)/shard_map/ppermute | solution.py:21
  115.5 5.3 %copy-start.13 = (f32[24]{0:T(128)S(1)}, f32[24]{0:T(128)}, u32[]{:S(2)}) copy-start(f32[24]{0:T(128)} %get-tuple-element.61) | copy-start | bytes 292
  120.8 1.1 copy-start.5
  120.8 2.1 %copy-start.4 = (f32[24,64,128]{2,1,0:T(8,128)S(1)}, f32[24,64,128]{2,1,0:T(8,128)}, u32[]{:S(2)}) copy-start(f32[24,64,128]{2,1,0:T(8,128)} %gather_fusion.3) | copy-start | bytes 2359300
  121.9 1.9 %copy-start.3 = (f32[24,64,128]{2,1,0:T(8,128)S(1)}, f32[24,64,128]{2,1,0:T(8,128)}, u32[]{:S(2)}) copy-start(f32[24,64,128]{2,1,0:T(8,128)} %gather_fusion.4) | copy-start | bytes 2359300
  122.8 1.9 %copy-start.15 = (f32[24]{0:T(128)S(1)}, f32[24]{0:T(128)}, u32[]{:S(2)}) copy-start(f32[24]{0:T(128)} %get-tuple-element.60) | copy-start | bytes 292
  124.7 0.9 copy-start.14
  125.6 1.1 copy-start.2
  125.7 1.1 copy-start.12
  132.9 4.9 %copy-start.6 = (s32[24,128]{1,0:T(8,128)S(1)}, s32[24,128]{1,0:T(8,128)}, u32[]{:S(2)}) copy-start(s32[24,128]{1,0:T(8,128)} %add_select_fusion.12) | copy-start | bytes 36868
  133.7 4.9 %copy-start.7 = (s32[24,128]{1,0:T(8,128)S(1)}, s32[24,128]{1,0:T(8,128)}, u32[]{:S(2)}) copy-start(s32[24,128]{1,0:T(8,128)} %add_select_fusion.11) | copy-start | bytes 36868
  134.5 4.9 %copy-start.8 = (s32[24,128]{1,0:T(8,128)S(1)}, s32[24,128]{1,0:T(8,128)}, u32[]{:S(2)}) copy-start(s32[24,128]{1,0:T(8,128)} %add_select_fusion.10) | copy-start | bytes 36868
  135.3 4.9 %copy-start.9 = (s32[24,128]{1,0:T(8,128)S(1)}, s32[24,128]{1,0:T(8,128)}, u32[]{:S(2)}) copy-start(s32[24,128]{1,0:T(8,128)} %add_select_fusion.14) | copy-start | bytes 36868
  136.2 4.9 %copy-start.10 = (s32[24,128]{1,0:T(8,128)S(1)}, s32[24,128]{1,0:T(8,128)}, u32[]{:S(2)}) copy-start(s32[24,128]{1,0:T(8,128)} %add_select_fusion.15) | copy-start | bytes 36868
  137.8 5.2 %copy-start.16 = (u32[32]{0:T(128)S(1)}, u32[32]{0:T(128)}, u32[]{:S(2)}) copy-start(u32[32]{0:T(128)} %constant.218) | copy-start | bytes 388
  142.6 6.4 %collective-permute-start.4 = (f32[21,128]{1,0:T(8,128)S(1)}, f32[21,128]{1,0:T(8,128)S(1)}, u32[]{:S(2)}, u32[]{:S(2)}) collective-permute-start(f32[21,128]{1,0:T(8,128)S(1)} %get-tuple-element.38), channel_id=1, source_target_pairs={{0,4},{4,8},{8,12},{12,16},{16,20},{20,24},{24,28},{28,0},{1,5},{5... | collective-permute-start | bytes 32264 | tf_op jit(solution)/shard_map/ppermute | solution.py:28
  144.2 5.9 %collective-permute-start.5 = (f32[21,128]{1,0:T(8,128)S(1)}, f32[21,128]{1,0:T(8,128)S(1)}, u32[]{:S(2)}, u32[]{:S(2)}) collective-permute-start(f32[21,128]{1,0:T(8,128)S(1)} %get-tuple-element.37), channel_id=1, source_target_pairs={{0,28},{4,0},{8,4},{12,8},{16,12},{20,16},{24,20},{28,24},{1,29},{... | collective-permute-start | bytes 32264 | tf_op jit(solution)/shard_map/ppermute | solution.py:28
Sparse Core Ops, SparseCore 0:
  39.4 26.7 all-gather.2
